TPU v7x, 256 devices: a whole 4x4x8 slice. The times are simulated.
256 devices in a mesh: seq: 32 (over y, x, core), head: 8 (over z).
Axes of the slice: x: 4, y: 4, z: 8, core: 2. Of those that a mesh axis runs over, the one named last changes fastest.
Arguments:
- queries: bfloat16 [32768, 8192], P(('seq', 'head')), may hold values from -6 to 6
- key_vectors: bfloat16 [32768, 8192], P(('seq', 'head')), may hold values from -6 to 6
- value_vectors: bfloat16 [32768, 8192], P(('seq', 'head')), may hold values from -6 to 6
- out_gain: float32 [64, 128], P('head'), may hold values from 0.1 to 1.9
Outputs:
- attended: bfloat16 [32768, 8192], P(('seq', 'head'))
All inputs are finite; a program needn't handle non-finite values.
Results may differ from a plain program's by a relative error of at most 0.0049.
Values may be sent and summed in bfloat16 or wider, within the bound.
A program may use at most 128 MiB of HBM per device.

v0:
```python
import jax
import jax.numpy as jnp
from jax import lax
from jax.sharding import PartitionSpec as P

HEADS = 64
HD = 128


def shifted(block, axis, distance):
    count = lax.axis_size(axis)
    return lax.ppermute(block, axis, [(i, i + distance) for i in range(count - distance)])


def seq_exclusive(own):
    count = lax.axis_size("seq")
    total = own
    distance = 1
    while distance < count:
        total = total + shifted(total, "seq", distance)
        distance *= 2
    return shifted(total, "seq", 1)


def per_device(queries, key_vectors, value_vectors, out_gain):
    tokens = queries.shape[0]
    query_heads = queries.reshape(tokens, HEADS, HD)
    key_heads = key_vectors.reshape(tokens, HEADS, HD)
    value_heads = value_vectors.reshape(tokens, HEADS, HD)
    states = jnp.einsum("bhd,bhe->hde", key_heads, value_heads, preferred_element_type=jnp.float32)
    gathered = lax.all_to_all(
        states.astype(jnp.bfloat16).reshape(8, HEADS // 8, HD, HD),
        "head",
        split_axis=0,
        concat_axis=0,
        tiled=True,
    ).astype(jnp.float32)
    gain = lax.all_gather(out_gain, "head", axis=0, tiled=True)
    prefix = seq_exclusive(jnp.sum(gathered, axis=0))
    running = prefix
    parts = []
    for z in range(8):
        parts.append(running.astype(jnp.bfloat16))
        running = running + gathered[z]
    carried = lax.all_to_all(jnp.stack(parts), "head", split_axis=0, concat_axis=0, tiled=True)
    carried = carried.reshape(HEADS, HD, HD)
    inter = jnp.einsum("bhd,hde->bhe", query_heads, carried, preferred_element_type=jnp.float32)
    scores = jnp.einsum("bhd,chd->hbc", query_heads, key_heads, preferred_element_type=jnp.float32)
    causal = jnp.arange(tokens)[:, None] >= jnp.arange(tokens)[None, :]
    scores = jnp.where(causal[None], scores, jnp.float32(0.0)).astype(jnp.bfloat16)
    intra = jnp.einsum("hbc,chd->bhd", scores, value_heads, preferred_element_type=jnp.float32)
    raw = inter + intra
    scale = lax.rsqrt(jnp.mean(raw * raw, axis=-1, keepdims=True) + 1e-06)
    normed = (raw * scale * gain[None]).astype(jnp.bfloat16)
    return normed.reshape(tokens, HEADS * HD)


def solution(mesh):
    return jax.shard_map(
        per_device,
        mesh=mesh,
        in_specs=(
            P(("seq", "head"), None),
            P(("seq", "head"), None),
            P(("seq", "head"), None),
            P("head", None),
        ),
        out_specs=P(("seq", "head"), None),
        check_vma=False,
    )
```

profile of v0, /device:TPU:56, one launch (start us, length us, event | category | flops | bytes accessed | tf_op | source)
XLA Modules:
  0.0 247.2 jit_solution(813136822619654408)
XLA Ops:
  0.0 4.2 %copy.11 = bf16[128,8192]{0,1:T(8,128)(2,1)} copy(bf16[128,8192]{1,0:T(8,128)(2,1)} %param.5) | data formatting | bytes 4194304 | tf_op jit(solution)/shard_map/reshape | solution.py:28
  4.2 4.1 %copy.12 = bf16[128,8192]{0,1:T(8,128)(2,1)} copy(bf16[128,8192]{1,0:T(8,128)(2,1)} %param.6) | data formatting | bytes 4194304 | tf_op jit(solution)/shard_map/reshape | solution.py:29
  8.3 3.8 %convolution_convert_fusion = bf16[64,128,128]{2,1,0:T(8,128)(2,1)S(1)} fusion(bf16[128,64,128]{0,2,1:T(8,128)(2,1)} %bitcast.108, bf16[128,64,128]{0,2,1:T(8,128)(2,1)} %bitcast.110), kind=kOutput, calls=%fused_computation.7 | convolution fusion | flops 269484032 | bytes 6291456 | tf_op jit(solution)/shard_map/bhd,bhe->hde/dot_general | solution.py:30
  12.1 58.1 %all_to_all.10 = bf16[8,8,128,128]{3,2,1,0:T(8,128)(2,1)S(1)} all-to-all(bf16[8,8,128,128]{3,2,1,0:T(8,128)(2,1)S(1)} %bitcast.113), channel_id=1, replica_groups=mesh['seq'=32,'head'=8] {'head'}, dimensions={0} | all-to-all | bytes 4194304 | tf_op jit(solution)/shard_map/all_to_all | solution.py:31
  70.5 1.9 collective-permute-start
  72.5 10.7 %collective-permute-done = f32[8,128,128]{2,1,0:T(8,128)S(1)} collective-permute-done((f32[8,128,128]{2,1,0:T(8,128)S(1)}, f32[8,128,128]{2,1,0:T(8,128)S(1)}, u32[]{:S(2)}, u32[]{:S(2)}) %collective-permute-start) | collective-permute-done | bytes 524320 | tf_op jit(solution)/shard_map/ppermute | solution.py:12
  83.2 1.9 collective-permute-start.1
  85.1 12.9 %collective-permute-done.1 = f32[8,128,128]{2,1,0:T(8,128)S(1)} collective-permute-done((f32[8,128,128]{2,1,0:T(8,128)S(1)}, f32[8,128,128]{2,1,0:T(8,128)S(1)}, u32[]{:S(2)}, u32[]{:S(2)}) %collective-permute-start.1) | collective-permute-done | bytes 524320 | tf_op jit(solution)/shard_map/ppermute | solution.py:12
  98.1 2.5 %collective-permute-start.2 = (f32[8,128,128]{2,1,0:T(8,128)S(1)}, f32[8,128,128]{2,1,0:T(8,128)S(1)}, u32[]{:S(2)}, u32[]{:S(2)}) collective-permute-start(f32[8,128,128]{2,1,0:T(8,128)S(1)} %add.51), channel_id=1, source_target_pairs={{0,32},{8,40},{16,48},{24,56},{32,64},{40,72},{48,80},{56,88},{64,... | collective-permute-start | bytes 1572872 | tf_op jit(solution)/shard_map/ppermute | solution.py:12
  100.7 11.8 %collective-permute-done.2 = f32[8,128,128]{2,1,0:T(8,128)S(1)} collective-permute-done((f32[8,128,128]{2,1,0:T(8,128)S(1)}, f32[8,128,128]{2,1,0:T(8,128)S(1)}, u32[]{:S(2)}, u32[]{:S(2)}) %collective-permute-start.2) | collective-permute-done | bytes 524320 | tf_op jit(solution)/shard_map/ppermute | solution.py:12
  112.5 1.3 collective-permute-start.3
  113.8 9.9 %collective-permute-done.3 = f32[8,128,128]{2,1,0:T(8,128)S(1)} collective-permute-done((f32[8,128,128]{2,1,0:T(8,128)S(1)}, f32[8,128,128]{2,1,0:T(8,128)S(1)}, u32[]{:S(2)}, u32[]{:S(2)}) %collective-permute-start.3) | collective-permute-done | bytes 524320 | tf_op jit(solution)/shard_map/ppermute | solution.py:12
  123.7 1.3 collective-permute-start.4
  125.0 11.3 %collective-permute-done.4 = f32[8,128,128]{2,1,0:T(8,128)S(1)} collective-permute-done((f32[8,128,128]{2,1,0:T(8,128)S(1)}, f32[8,128,128]{2,1,0:T(8,128)S(1)}, u32[]{:S(2)}, u32[]{:S(2)}) %collective-permute-start.4) | collective-permute-done | bytes 524320 | tf_op jit(solution)/shard_map/ppermute | solution.py:12
  136.3 1.9 collective-permute-start.5
  138.8 10.2 %collective-permute-done.5 = f32[8,128,128]{2,1,0:T(8,128)S(1)} collective-permute-done((f32[8,128,128]{2,1,0:T(8,128)S(1)}, f32[8,128,128]{2,1,0:T(8,128)S(1)}, u32[]{:S(2)}, u32[]{:S(2)}) %collective-permute-start.5) | collective-permute-done | bytes 524320 | tf_op jit(solution)/shard_map/ppermute | solution.py:12
  152.0 0.8 bitcast_dynamic-update-slice_fusion.2
  154.4 0.8 fusion.16
  155.2 5.8 %all-to-all-start.1 = ((bf16[8,8,128,128]{3,2,1,0:T(8,128)(2,1)}), bf16[8,8,128,128]{3,2,1,0:T(8,128)(2,1)}, u32[]{:S(2)}, u32[]{:S(2)}) async-start(bf16[8,8,128,128]{3,2,1,0:T(8,128)(2,1)} %fusion.16), calls=%async_computation.1 | async-start | bytes 4194304 | tf_op jit(solution)/shard_map/all_to_all | solution.py:45
  161.0 65.5 %all_gather.3 = f32[64,128]{1,0:T(8,128)S(1)} all-gather(f32[8,128]{1,0:T(8,128)S(1)} %copy-done.1), channel_id=1, replica_groups=mesh['seq'=32,'head'=8] {'head'}, dimensions={0}, use_global_device_ids=true | all-gather | bytes 36864 | tf_op jit(solution)/shard_map/all_gather | solution.py:38
  226.5 5.1 %fusion.1 = f32[64,128,128]{2,1,0:T(8,128)} fusion(bf16[64,128,128]{2,1,0:T(8,128)(2,1)} %bitcast.21, bf16[128,8192]{1,0:T(8,128)(2,1)S(1)} %copy-done), kind=kOutput, calls=%fused_computation.5 | convolution fusion | flops 268435456 | bytes 8388608 | tf_op jit(solution)/shard_map/bhd,hde->bhe/dot_general | solution.py:47
  231.7 7.6 %multiply_reduce_fusion = (f32[128,64]{0,1:T(8,128)S(1)}, f32[128,64,128]{0,2,1:T(8,128)}) fusion(bf16[128,64,128]{0,2,1:T(8,128)(2,1)} %bitcast.111, bf16[128,64,128]{0,2,1:T(8,128)(2,1)} %bitcast.109, pred[128,128]{1,0:T(8,128)(4,1)S(1)} %iota_compare_fusion, f32[64,128,128]{2,1,0:T(8,128)} %fusion.1, bf16[128,8192]{1,0:T(8,128)(2,1)S(1)} %copy-done), kind=kOutput, calls=%fused_computation.2 | convolution fusion | flops 542105600 | bytes 14729216 | tf_op jit(solution)/shard_map/hbc,chd->bhd/dot_general | solution.py:51
  239.2 3.9 %multiply_convert_fusion = bf16[128,64,128]{0,2,1:T(8,128)(2,1)} fusion(f32[128,64,128]{0,2,1:T(8,128)} %get-tuple-element.10, f32[64,128]{1,0:T(8,128)S(1)} %all_gather.3, f32[128,64]{0,1:T(8,128)S(1)} %add_rsqrt_fusion), kind=kLoop, calls=%fused_computation.1 | loop fusion | flops 3145728 | bytes 6356992 | tf_op jit(solution)/shard_map/convert_element_type | solution.py:54
  243.1 4.1 %copy.10 = bf16[128,8192]{1,0:T(8,128)(2,1)} copy(bf16[128,8192]{0,1:T(8,128)(2,1)} %bitcast.112) | data formatting | bytes 4194304 | tf_op jit(solution)/shard_map/reshape | solution.py:55
  (20 shorter events, 5.8 us)
Async XLA Ops:
  0.0 226.5 %copy-start = (bf16[128,8192]{1,0:T(8,128)(2,1)S(1)}, bf16[128,8192]{1,0:T(8,128)(2,1)}, u32[]{:S(2)}) copy-start(bf16[128,8192]{1,0:T(8,128)(2,1)} %param.4) | copy-start | bytes 6291460
  70.5 12.6 %collective-permute-start = (f32[8,128,128]{2,1,0:T(8,128)S(1)}, f32[8,128,128]{2,1,0:T(8,128)S(1)}, u32[]{:S(2)}, u32[]{:S(2)}) collective-permute-start(f32[8,128,128]{2,1,0:T(8,128)S(1)} %convert_reduce_fusion), channel_id=1, source_target_pairs={{0,8},{8,16},{16,24},{24,32},{32,40},{40,48},{48,56},{56,64},{64,7... | collective-permute-start | bytes 1572872 | tf_op jit(solution)/shard_map/ppermute | solution.py:12
  83.2 14.8 %collective-permute-start.1 = (f32[8,128,128]{2,1,0:T(8,128)S(1)}, f32[8,128,128]{2,1,0:T(8,128)S(1)}, u32[]{:S(2)}, u32[]{:S(2)}) collective-permute-start(f32[8,128,128]{2,1,0:T(8,128)S(1)} %add.50), channel_id=1, source_target_pairs={{0,16},{8,24},{16,32},{24,40},{32,48},{40,56},{48,64},{56,72},{64,... | collective-permute-start | bytes 1572872 | tf_op jit(solution)/shard_map/ppermute | solution.py:12
  98.1 14.3 %collective-permute-start.2 = (f32[8,128,128]{2,1,0:T(8,128)S(1)}, f32[8,128,128]{2,1,0:T(8,128)S(1)}, u32[]{:S(2)}, u32[]{:S(2)}) collective-permute-start(f32[8,128,128]{2,1,0:T(8,128)S(1)} %add.51), channel_id=1, source_target_pairs={{0,32},{8,40},{16,48},{24,56},{32,64},{40,72},{48,80},{56,88},{64,... | collective-permute-start | bytes 1572872 | tf_op jit(solution)/shard_map/ppermute | solution.py:12
  112.5 11.2 %collective-permute-start.3 = (f32[8,128,128]{2,1,0:T(8,128)S(1)}, f32[8,128,128]{2,1,0:T(8,128)S(1)}, u32[]{:S(2)}, u32[]{:S(2)}) collective-permute-start(f32[8,128,128]{2,1,0:T(8,128)S(1)} %add.52), channel_id=1, source_target_pairs={{0,64},{8,72},{16,80},{24,88},{32,96},{40,104},{48,112},{56,120},{... | collective-permute-start | bytes 1572872 | tf_op jit(solution)/shard_map/ppermute | solution.py:12
  123.7 12.6 %collective-permute-start.4 = (f32[8,128,128]{2,1,0:T(8,128)S(1)}, f32[8,128,128]{2,1,0:T(8,128)S(1)}, u32[]{:S(2)}, u32[]{:S(2)}) collective-permute-start(f32[8,128,128]{2,1,0:T(8,128)S(1)} %add.53), channel_id=1, source_target_pairs={{0,128},{8,136},{16,144},{24,152},{32,160},{40,168},{48,176},{56,1... | collective-permute-start | bytes 1572872 | tf_op jit(solution)/shard_map/ppermute | solution.py:12
  136.3 12.6 %collective-permute-start.5 = (f32[8,128,128]{2,1,0:T(8,128)S(1)}, f32[8,128,128]{2,1,0:T(8,128)S(1)}, u32[]{:S(2)}, u32[]{:S(2)}) collective-permute-start(f32[8,128,128]{2,1,0:T(8,128)S(1)} %add.54), channel_id=1, source_target_pairs={{0,8},{8,16},{16,24},{24,32},{32,40},{40,48},{48,56},{56,64},{64,7... | collective-permute-start | bytes 1572872 | tf_op jit(solution)/shard_map/ppermute | solution.py:12
  155.2 5.8 %copy-start.1 = (f32[8,128]{1,0:T(8,128)S(1)}, f32[8,128]{1,0:T(8,128)}, u32[]{:S(2)}) copy-start(f32[8,128]{1,0:T(8,128)} %param.7) | copy-start | bytes 12292
  155.2 71.3 %all-to-all-start.1 = ((bf16[8,8,128,128]{3,2,1,0:T(8,128)(2,1)}), bf16[8,8,128,128]{3,2,1,0:T(8,128)(2,1)}, u32[]{:S(2)}, u32[]{:S(2)}) async-start(bf16[8,8,128,128]{3,2,1,0:T(8,128)(2,1)} %fusion.16), calls=%async_computation.1 | async-start | bytes 4194304 | tf_op jit(solution)/shard_map/all_to_all | solution.py:45
where the time goes:
time: 248 us; the launch traced here: 247 us
  blocking collectives  124 us (50%)
  waiting for transfers between devices  66.7 us (27%)
  starting transfers between devices  16.7 us (7%)
  matrix products  16.5 us (7%)
  local copies, waits for them, and re-layouts  12.3 us (5%)
  other arithmetic  11.3 us (5%)
    ppermute x6, waiting for transfers between devices, shifted(): lax.ppermute(block, axis, [(i, i + distance) for i in range(count - dista...  66.7 us
    all_gather x1, blocking collectives, per_device(): gain = lax.all_gather(out_gain, 'head', axis=0, tiled=True)  65.5 us
    all_to_all x1, blocking collectives, per_device(): lax.all_to_all(states.astype(jnp.bfloat16).reshape(8, HEADS // 8, HD, HD)...  58.1 us
    ppermute x6, starting transfers between devices, shifted(): lax.ppermute(block, axis, [(i, i + distance) for i in range(count - dista...  10.9 us
    dot_general x1, matrix products, per_device(): jnp.einsum('hbc,chd->bhd', scores, value_heads, preferred_element_type=jn...  7.56 us
    all_to_all x1, starting transfers between devices, per_device(): lax.all_to_all(jnp.stack(parts), 'head', split_axis=0, concat_axis=0, til...  5.8 us
    unnamed x7, other arithmetic  5.4 us
    dot_general x1, matrix products, per_device(): jnp.einsum('bhd,hde->bhe', query_heads, carried, preferred_element_type=j...  5.14 us
  transfers between devices with their start and end apart: 7, of which 6 were waited for; matrix products, arithmetic and copies ran while one was open for 0% of the time, Pallas kernels for 0%

commit v1 on v0

--- a/solution.py
+++ b/solution.py
@@ -35,7 +35,9 @@
         concat_axis=0,
         tiled=True,
     ).astype(jnp.float32)
-    gain = lax.all_gather(out_gain, "head", axis=0, tiled=True)
+    gain = jnp.concatenate(
+        lax.all_to_all(jnp.stack([out_gain] * lax.axis_size("head")), "head", 0, 0), axis=0
+    )
     prefix = seq_exclusive(jnp.sum(gathered, axis=0))
     running = prefix
     parts = []

time: 248 us -> 236 us (0.952)
  blocking collectives: 124 us -> 58.1 us
  waiting for transfers between devices: 66.7 us -> 115 us
  starting transfers between devices: 16.7 us -> 21.4 us
    all_gather x1 -> x0, blocking collectives: 65.5 us -> none  [per_device(): gain = lax.all_gather(out_gain, 'head', axis=0, tiled=True)]
    all_to_all x1, waiting for transfers between devices: 0.01 us -> 48.6 us  [per_device(): lax.all_to_all(jnp.stack(parts), 'head', split_axis=0, concat_axis=0, til...]
    all_to_all x0 -> x1, starting transfers between devices: none -> 4.73 us  [per_device(): lax.all_to_all(jnp.stack([out_gain] * lax.axis_size('head')), 'head', 0, 0)]
  transfers between devices with their start and end apart: 7 -> 8, of which waited for: 6 -> 7; matrix products, arithmetic and copies ran while one was open for 0% -> 6% of each run, Pallas kernels for 0% -> 0%
where the time goes in v1:
time: 236 us
  waiting for transfers between devices  115 us (49%)
  blocking collectives  58.1 us (25%)
  starting transfers between devices  21.4 us (9%)
  matrix products  16.5 us (7%)
  local copies, waits for them, and re-layouts  13 us (6%)
  other arithmetic  11.3 us (5%)
    ppermute x6, waiting for transfers between devices, shifted(): lax.ppermute(block, axis, [(i, i + distance) for i in range(count - dista...  66.7 us
    all_to_all x1, blocking collectives, per_device(): lax.all_to_all(states.astype(jnp.bfloat16).reshape(8, HEADS // 8, HD, HD)...  58.1 us
    all_to_all x1, waiting for transfers between devices, per_device(): lax.all_to_all(jnp.stack(parts), 'head', split_axis=0, concat_axis=0, til...  48.6 us
    ppermute x6, starting transfers between devices, shifted(): lax.ppermute(block, axis, [(i, i + distance) for i in range(count - dista...  10.9 us
    dot_general x1, matrix products, per_device(): jnp.einsum('hbc,chd->bhd', scores, value_heads, preferred_element_type=jn...  7.56 us
    all_to_all x1, starting transfers between devices, per_device(): lax.all_to_all(jnp.stack(parts), 'head', split_axis=0, concat_axis=0, til...  5.81 us
    unnamed x7, other arithmetic  5.43 us
    dot_general x1, matrix products, per_device(): jnp.einsum('bhd,hde->bhe', query_heads, carried, preferred_element_type=j...  5.15 us
  transfers between devices with their start and end apart: 8, of which 7 were waited for; matrix products, arithmetic and copies ran while one was open for 6% of the time, Pallas kernels for 0%

profile of v1, /device:TPU:56, one launch (start us, length us, event | category | flops | bytes accessed | tf_op | source)
XLA Modules:
  0.0 235.6 jit_solution(2183062496052886105)
XLA Ops:
  0.0 4.2 %copy.11 = bf16[128,8192]{0,1:T(8,128)(2,1)} copy(bf16[128,8192]{1,0:T(8,128)(2,1)} %param.5) | data formatting | bytes 4194304 | tf_op jit(solution)/shard_map/reshape | solution.py:28
  4.2 4.1 %copy.12 = bf16[128,8192]{0,1:T(8,128)(2,1)} copy(bf16[128,8192]{1,0:T(8,128)(2,1)} %param.6) | data formatting | bytes 4194304 | tf_op jit(solution)/shard_map/reshape | solution.py:29
  8.3 3.8 %convolution_convert_fusion = bf16[64,128,128]{2,1,0:T(8,128)(2,1)S(1)} fusion(bf16[128,64,128]{0,2,1:T(8,128)(2,1)} %bitcast.109, bf16[128,64,128]{0,2,1:T(8,128)(2,1)} %bitcast.111), kind=kOutput, calls=%fused_computation.7 | convolution fusion | flops 269484032 | bytes 6291456 | tf_op jit(solution)/shard_map/bhd,bhe->hde/dot_general | solution.py:30
  12.1 58.1 %all_to_all.15 = bf16[8,8,128,128]{3,2,1,0:T(8,128)(2,1)S(1)} all-to-all(bf16[8,8,128,128]{3,2,1,0:T(8,128)(2,1)S(1)} %bitcast.114), channel_id=1, replica_groups=mesh['seq'=32,'head'=8] {'head'}, dimensions={0} | all-to-all | bytes 4194304 | tf_op jit(solution)/shard_map/all_to_all | solution.py:31
  70.5 1.9 collective-permute-start
  72.5 10.7 %collective-permute-done = f32[8,128,128]{2,1,0:T(8,128)S(1)} collective-permute-done((f32[8,128,128]{2,1,0:T(8,128)S(1)}, f32[8,128,128]{2,1,0:T(8,128)S(1)}, u32[]{:S(2)}, u32[]{:S(2)}) %collective-permute-start) | collective-permute-done | bytes 524320 | tf_op jit(solution)/shard_map/ppermute | solution.py:12
  83.2 1.9 collective-permute-start.1
  85.1 12.9 %collective-permute-done.1 = f32[8,128,128]{2,1,0:T(8,128)S(1)} collective-permute-done((f32[8,128,128]{2,1,0:T(8,128)S(1)}, f32[8,128,128]{2,1,0:T(8,128)S(1)}, u32[]{:S(2)}, u32[]{:S(2)}) %collective-permute-start.1) | collective-permute-done | bytes 524320 | tf_op jit(solution)/shard_map/ppermute | solution.py:12
  98.1 2.5 %collective-permute-start.2 = (f32[8,128,128]{2,1,0:T(8,128)S(1)}, f32[8,128,128]{2,1,0:T(8,128)S(1)}, u32[]{:S(2)}, u32[]{:S(2)}) collective-permute-start(f32[8,128,128]{2,1,0:T(8,128)S(1)} %add.51), channel_id=1, source_target_pairs={{0,32},{8,40},{16,48},{24,56},{32,64},{40,72},{48,80},{56,88},{64,... | collective-permute-start | bytes 1572872 | tf_op jit(solution)/shard_map/ppermute | solution.py:12
  100.7 11.8 %collective-permute-done.2 = f32[8,128,128]{2,1,0:T(8,128)S(1)} collective-permute-done((f32[8,128,128]{2,1,0:T(8,128)S(1)}, f32[8,128,128]{2,1,0:T(8,128)S(1)}, u32[]{:S(2)}, u32[]{:S(2)}) %collective-permute-start.2) | collective-permute-done | bytes 524320 | tf_op jit(solution)/shard_map/ppermute | solution.py:12
  112.5 1.3 collective-permute-start.3
  113.8 9.9 %collective-permute-done.3 = f32[8,128,128]{2,1,0:T(8,128)S(1)} collective-permute-done((f32[8,128,128]{2,1,0:T(8,128)S(1)}, f32[8,128,128]{2,1,0:T(8,128)S(1)}, u32[]{:S(2)}, u32[]{:S(2)}) %collective-permute-start.3) | collective-permute-done | bytes 524320 | tf_op jit(solution)/shard_map/ppermute | solution.py:12
  123.7 1.3 collective-permute-start.4
  125.0 11.3 %collective-permute-done.4 = f32[8,128,128]{2,1,0:T(8,128)S(1)} collective-permute-done((f32[8,128,128]{2,1,0:T(8,128)S(1)}, f32[8,128,128]{2,1,0:T(8,128)S(1)}, u32[]{:S(2)}, u32[]{:S(2)}) %collective-permute-start.4) | collective-permute-done | bytes 524320 | tf_op jit(solution)/shard_map/ppermute | solution.py:12
  136.3 1.9 collective-permute-start.5
  138.8 10.2 %collective-permute-done.5 = f32[8,128,128]{2,1,0:T(8,128)S(1)} collective-permute-done((f32[8,128,128]{2,1,0:T(8,128)S(1)}, f32[8,128,128]{2,1,0:T(8,128)S(1)}, u32[]{:S(2)}, u32[]{:S(2)}) %collective-permute-start.5) | collective-permute-done | bytes 524320 | tf_op jit(solution)/shard_map/ppermute | solution.py:12
  154.4 0.8 fusion.16
  155.2 5.8 %all-to-all-start.1 = ((bf16[8,8,128,128]{3,2,1,0:T(8,128)(2,1)}), bf16[8,8,128,128]{3,2,1,0:T(8,128)(2,1)}, u32[]{:S(2)}, u32[]{:S(2)}) async-start(bf16[8,8,128,128]{3,2,1,0:T(8,128)(2,1)} %fusion.16), calls=%async_computation.1 | async-start | bytes 4194304 | tf_op jit(solution)/shard_map/all_to_all | solution.py:47
  161.1 48.6 %all-to-all-done.1 = bf16[8,8,128,128]{3,2,1,0:T(8,128)(2,1)} async-done(((bf16[8,8,128,128]{3,2,1,0:T(8,128)(2,1)}), bf16[8,8,128,128]{3,2,1,0:T(8,128)(2,1)}, u32[]{:S(2)}, u32[]{:S(2)}) %all-to-all-start.1) | async-done | bytes 2097184 | tf_op jit(solution)/shard_map/all_to_all | solution.py:47
  210.2 4.7 %all-to-all-start.2 = ((f32[8,8,128]{2,1,0:T(8,128)}), f32[8,8,128]{2,1,0:T(8,128)S(1)}, u32[]{:S(2)}, u32[]{:S(2)}) async-start(f32[8,8,128]{2,1,0:T(8,128)} %stack.47), calls=%async_computation.2 | async-start | bytes 65536 | tf_op jit(solution)/shard_map/all_to_all | solution.py:39
  215.0 5.2 %fusion.1 = f32[64,128,128]{2,1,0:T(8,128)} fusion(bf16[64,128,128]{2,1,0:T(8,128)(2,1)} %bitcast.22, bf16[128,8192]{1,0:T(8,128)(2,1)S(1)} %copy-done), kind=kOutput, calls=%fused_computation.5 | convolution fusion | flops 268435456 | bytes 8388608 | tf_op jit(solution)/shard_map/bhd,hde->bhe/dot_general | solution.py:49
  220.1 7.6 %multiply_reduce_fusion = (f32[128,64]{0,1:T(8,128)S(1)}, f32[128,64,128]{0,2,1:T(8,128)}) fusion(bf16[128,64,128]{0,2,1:T(8,128)(2,1)} %bitcast.112, bf16[128,64,128]{0,2,1:T(8,128)(2,1)} %bitcast.110, pred[128,128]{1,0:T(8,128)(4,1)S(1)} %iota_compare_fusion, f32[64,128,128]{2,1,0:T(8,128)} %fusion.1, bf16[128,8192]{1,0:T(8,128)(2,1)S(1)} %copy-done), kind=kOutput, calls=%fused_computation.2 | convolution fusion | flops 542105600 | bytes 14729216 | tf_op jit(solution)/shard_map/hbc,chd->bhd/dot_general | solution.py:53
  227.7 3.8 %multiply_convert_fusion = bf16[128,64,128]{0,2,1:T(8,128)(2,1)} fusion(f32[128,64,128]{0,2,1:T(8,128)} %get-tuple-element.10, f32[64,128]{1,0:T(8,128)S(1)} %bitcast.115, f32[128,64]{0,1:T(8,128)S(1)} %add_rsqrt_fusion), kind=kLoop, calls=%fused_computation.1 | loop fusion | flops 3145728 | bytes 6356992 | tf_op jit(solution)/shard_map/convert_element_type | solution.py:56
  231.6 4.1 %copy.10 = bf16[128,8192]{1,0:T(8,128)(2,1)} copy(bf16[128,8192]{0,1:T(8,128)(2,1)} %bitcast.113) | data formatting | bytes 4194304 | tf_op jit(solution)/shard_map/reshape | solution.py:57
  (22 shorter events, 7.2 us)
Async XLA Ops:
  0.0 215.0 %copy-start = (bf16[128,8192]{1,0:T(8,128)(2,1)S(1)}, bf16[128,8192]{1,0:T(8,128)(2,1)}, u32[]{:S(2)}) copy-start(bf16[128,8192]{1,0:T(8,128)(2,1)} %param.4) | copy-start | bytes 6291460
  70.5 12.6 %collective-permute-start = (f32[8,128,128]{2,1,0:T(8,128)S(1)}, f32[8,128,128]{2,1,0:T(8,128)S(1)}, u32[]{:S(2)}, u32[]{:S(2)}) collective-permute-start(f32[8,128,128]{2,1,0:T(8,128)S(1)} %convert_reduce_fusion), channel_id=1, source_target_pairs={{0,8},{8,16},{16,24},{24,32},{32,40},{40,48},{48,56},{56,64},{64,7... | collective-permute-start | bytes 1572872 | tf_op jit(solution)/shard_map/ppermute | solution.py:12
  83.2 14.8 %collective-permute-start.1 = (f32[8,128,128]{2,1,0:T(8,128)S(1)}, f32[8,128,128]{2,1,0:T(8,128)S(1)}, u32[]{:S(2)}, u32[]{:S(2)}) collective-permute-start(f32[8,128,128]{2,1,0:T(8,128)S(1)} %add.50), channel_id=1, source_target_pairs={{0,16},{8,24},{16,32},{24,40},{32,48},{40,56},{48,64},{56,72},{64,... | collective-permute-start | bytes 1572872 | tf_op jit(solution)/shard_map/ppermute | solution.py:12
  98.1 14.3 %collective-permute-start.2 = (f32[8,128,128]{2,1,0:T(8,128)S(1)}, f32[8,128,128]{2,1,0:T(8,128)S(1)}, u32[]{:S(2)}, u32[]{:S(2)}) collective-permute-start(f32[8,128,128]{2,1,0:T(8,128)S(1)} %add.51), channel_id=1, source_target_pairs={{0,32},{8,40},{16,48},{24,56},{32,64},{40,72},{48,80},{56,88},{64,... | collective-permute-start | bytes 1572872 | tf_op jit(solution)/shard_map/ppermute | solution.py:12
  112.5 11.2 %collective-permute-start.3 = (f32[8,128,128]{2,1,0:T(8,128)S(1)}, f32[8,128,128]{2,1,0:T(8,128)S(1)}, u32[]{:S(2)}, u32[]{:S(2)}) collective-permute-start(f32[8,128,128]{2,1,0:T(8,128)S(1)} %add.52), channel_id=1, source_target_pairs={{0,64},{8,72},{16,80},{24,88},{32,96},{40,104},{48,112},{56,120},{... | collective-permute-start | bytes 1572872 | tf_op jit(solution)/shard_map/ppermute | solution.py:12
  123.7 12.6 %collective-permute-start.4 = (f32[8,128,128]{2,1,0:T(8,128)S(1)}, f32[8,128,128]{2,1,0:T(8,128)S(1)}, u32[]{:S(2)}, u32[]{:S(2)}) collective-permute-start(f32[8,128,128]{2,1,0:T(8,128)S(1)} %add.53), channel_id=1, source_target_pairs={{0,128},{8,136},{16,144},{24,152},{32,160},{40,168},{48,176},{56,1... | collective-permute-start | bytes 1572872 | tf_op jit(solution)/shard_map/ppermute | solution.py:12
  136.3 12.6 %collective-permute-start.5 = (f32[8,128,128]{2,1,0:T(8,128)S(1)}, f32[8,128,128]{2,1,0:T(8,128)S(1)}, u32[]{:S(2)}, u32[]{:S(2)}) collective-permute-start(f32[8,128,128]{2,1,0:T(8,128)S(1)} %add.54), channel_id=1, source_target_pairs={{0,8},{8,16},{16,24},{24,32},{32,40},{40,48},{48,56},{56,64},{64,7... | collective-permute-start | bytes 1572872 | tf_op jit(solution)/shard_map/ppermute | solution.py:12
  155.2 54.4 %copy-start.1 = (f32[8,128]{1,0:T(8,128)S(1)}, f32[8,128]{1,0:T(8,128)}, u32[]{:S(2)}) copy-start(f32[8,128]{1,0:T(8,128)} %param.7) | copy-start | bytes 12292
  155.2 54.4 %all-to-all-start.1 = ((bf16[8,8,128,128]{3,2,1,0:T(8,128)(2,1)}), bf16[8,8,128,128]{3,2,1,0:T(8,128)(2,1)}, u32[]{:S(2)}, u32[]{:S(2)}) async-start(bf16[8,8,128,128]{3,2,1,0:T(8,128)(2,1)} %fusion.16), calls=%async_computation.1 | async-start | bytes 4194304 | tf_op jit(solution)/shard_map/all_to_all | solution.py:47
  210.2 17.5 %all-to-all-start.2 = ((f32[8,8,128]{2,1,0:T(8,128)}), f32[8,8,128]{2,1,0:T(8,128)S(1)}, u32[]{:S(2)}, u32[]{:S(2)}) async-start(f32[8,8,128]{2,1,0:T(8,128)} %stack.47), calls=%async_computation.2 | async-start | bytes 65536 | tf_op jit(solution)/shard_map/all_to_all | solution.py:39
